TPU v7x, 512 devices: a whole 4x4x16 slice. The times are simulated.
512 devices in a mesh: blk: 32 (over z, core), env: 16 (over y, x).
Axes of the slice: x: 4, y: 4, z: 16, core: 2. Of those that a mesh axis runs over, the one named last changes fastest.
Arguments:
- psi: float32 [4096, 1024], P('blk', 'env')
- env_left: bfloat16 [4096, 16, 1024], P('blk', 'env')
- env_right: bfloat16 [16, 1024, 1024], P('env')
- sector_tiles: int32 [16], replicated, may hold values from 1 to 8, as said below
- pairing: int32 [16, 16], replicated, may hold values from 0 to 15, as said below
- coupling: int32 [16, 16], replicated, may hold values from 0 to 1, as said below
Outputs:
- products: float32 [3, 4096, 1024], P(None, 'blk', 'env')
- quotients: float32 [3], replicated
- next_vector: float32 [4096, 1024], P('blk', 'env')
Inputs may be any that keep to these rules, and one draw needn't show every extreme that they name: Sector k covers tiles first_tile[k] to first_tile[k] + sector_tiles[k] - 1 of 128 rows; together the sectors cover all 32 tiles. Channel 0 maps every sector to itself: pairing[k, 0] = k. Channel 0 acts on every sector: coupling[k, 0] = 1.
All inputs are finite; a program needn't handle non-finite values.
Results may differ from a plain program's by a relative error of at most 0.0091.
Values may be sent and summed in bfloat16 or wider, within the bound.
No kernel may reach another device: no remote copies, remote signals or barrier semaphores. Data moves between devices by JAX's collectives and lax.ppermute only.
A program may use at most 64 MiB of HBM per device.

v0:
```python
import jax
import jax.numpy as jnp
from jax import lax
from jax.sharding import PartitionSpec as P

TILE = 128
ITERS = 3
EPSILON = 1e-06


def lookup_sources(sector_tiles, pairing, coupling, tile_ids, source_span):
    first_tile = jnp.cumsum(sector_tiles) - sector_tiles
    sector_ids = jnp.arange(sector_tiles.shape[0], dtype=jnp.int32)
    sector_of = jnp.sum((tile_ids[:, None] >= first_tile[None, :]).astype(jnp.int32), axis=1) - 1
    sector_pick = (sector_of[:, None] == sector_ids[None, :]).astype(jnp.int32)
    source_sector = jnp.sum(sector_pick[:, :, None] * pairing[None, :, :], axis=1)
    coupled = jnp.sum(sector_pick[:, :, None] * coupling[None, :, :], axis=1)
    source_pick = (source_sector[:, :, None] == sector_ids[None, None, :]).astype(jnp.int32)
    source_first = jnp.sum(source_pick * first_tile[None, None, :], axis=2) * TILE
    source_rows = jnp.sum(source_pick * sector_tiles[None, None, :], axis=2) * TILE
    offsets = jnp.arange(source_span, dtype=jnp.int32)
    keep_mask = (offsets[None, None, :] < source_rows[:, :, None]) & (coupled[:, :, None] == 1)
    return (source_first, keep_mask)


def per_device(psi, env_left, env_right, sector_tiles, pairing, coupling):
    row_count, col_width = psi.shape
    env_count = lax.axis_size("env")
    blk_count = lax.axis_size("blk")
    tile_local = row_count // TILE
    source_span = env_left.shape[2]
    local_terms = env_right.shape[0]
    all_terms = pairing.shape[1]
    full_width = col_width * env_count
    tile_ids = lax.axis_index("blk") * tile_local + jnp.arange(tile_local, dtype=jnp.int32)
    source_first, keep_mask = lookup_sources(sector_tiles, pairing, coupling, tile_ids, source_span)
    start_list = jnp.transpose(source_first).reshape(-1)
    term_first = lax.axis_index("env") * local_terms
    local_keep = lax.dynamic_slice_in_dim(keep_mask, term_first, local_terms, 1)
    left_panel = jnp.where(
        local_keep[:, None], env_left.reshape(tile_local, TILE, local_terms, source_span), 0
    )
    entry_count = float(row_count * blk_count * full_width)
    vector = psi
    product_list = []
    quotient_list = []
    for iteration in range(ITERS):
        rounded = vector.astype(jnp.bfloat16)
        every_row = lax.all_gather(rounded, "blk", axis=0, tiled=True)
        padded = jnp.concatenate(
            [every_row, jnp.zeros((source_span, col_width), jnp.bfloat16)], axis=0
        )
        source_slabs = jax.vmap(
            lambda first_row: lax.dynamic_slice_in_dim(padded, first_row, source_span, 0)
        )(start_list)
        source_slabs = source_slabs.reshape(all_terms, tile_local, source_span, col_width)
        moved_rows = lax.all_to_all(source_slabs, "env", split_axis=0, concat_axis=3, tiled=True)
        channel_mix = jnp.einsum(
            "dxtj,tdjc->tdxc", left_panel, moved_rows, preferred_element_type=jnp.float32
        )
        channel_mix = channel_mix.astype(jnp.bfloat16).reshape(local_terms, row_count, full_width)
        partial_sum = jnp.einsum(
            "trb,tbc->rc", channel_mix, env_right, preferred_element_type=jnp.float32
        )
        summed_all = lax.psum(partial_sum, "env")
        product = lax.dynamic_slice_in_dim(
            summed_all, lax.axis_index("env") * col_width, col_width, 1
        )
        inner_sum, square_sum = lax.psum(
            (jnp.sum(vector * product), jnp.sum(vector * vector)), ("blk", "env")
        )
        quotient = inner_sum / square_sum
        residual = product - quotient * vector
        energy = lax.psum(jnp.sum(residual * residual), ("blk", "env"))
        vector = residual * lax.rsqrt(energy / entry_count + EPSILON)
        product_list.append(product)
        quotient_list.append(quotient)
    return (jnp.stack(product_list), jnp.stack(quotient_list), vector)


def solution(mesh):
    placed = (P("blk", "env"), P("blk", "env", None), P("env", None, None), P(), P(), P())
    return jax.shard_map(
        per_device,
        mesh=mesh,
        in_specs=placed,
        out_specs=(P(None, "blk", "env"), P(), P("blk", "env")),
        check_vma=False,
    )
```

profile of v0, /device:TPU:1, one launch (start us, length us, event | category | flops | bytes accessed | tf_op | source)
XLA Modules:
  0.0 1310.4 jit_solution(9975891204792734560)
XLA Ops:
  7.2 0.9 copy.34
  8.2 1.3 fusion.18
  10.2 0.8 multiply_reduce_fusion.9
  11.0 0.8 select_reduce_fusion.1
  11.8 0.8 convert_element_type.39
  12.6 39.0 %all_gather.9 = bf16[4096,64]{0,1:T(8,128)(2,1)S(1)} all-gather(bf16[128,64]{0,1:T(8,128)(2,1)S(1)} %convert_element_type.39), channel_id=1, replica_groups=mesh['blk'=32,'env'=16] {'blk'}, dimensions={0}, use_global_device_ids=true | all-gather | bytes 540672 | tf_op jit(solution)/shard_map/all_gather | solution.py:49
  51.6 1.6 broadcast.241.clone2
  53.2 37.1 %while.3 = (s32[]{:T(128)}, bf16[5120,64]{0,1:T(8,128)(2,1)S(1)}, s32[16,2]{0,1:T(2,128)S(1)}, bf16[16,1024,64]{1,2,0:T(8,128)(2,1)}, s32[]{:T(128)}) while((s32[]{:T(128)}, bf16[5120,64]{0,1:T(8,128)(2,1)S(1)}, s32[16,2]{0,1:T(2,128)S(1)}, bf16[16,1024,64]{1,2,0:T(8,128)(2,1)}, s32[]{:T(128)}) %tuple.64), condition=%wide.while_cond, body=%wide.while_body.sunk | while | flops 2 | bytes 1049181 | solution.py:54
  56.1 0.8 constant_dynamic-slice_fusion.13
  60.7 0.8 constant_dynamic-slice_fusion.13
  63.1 0.8 constant_dynamic-slice_fusion.13
  65.4 0.8 constant_dynamic-slice_fusion.13
  67.7 0.8 constant_dynamic-slice_fusion.13
  79.3 0.8 constant_dynamic-slice_fusion.13
  86.3 0.8 constant_dynamic-slice_fusion.13
  90.3 6.9 all-to-all-start
  98.5 1.3 and_reduce_fusion
  99.8 30.3 %all-to-all-done = bf16[16,1,1024,64]{2,3,1,0:T(8,128)(2,1)} async-done(((bf16[16,1,1024,64]{2,3,1,0:T(8,128)(2,1)}), bf16[16,1,1024,64]{2,3,1,0:T(8,128)(2,1)}, u32[]{:S(2)}, u32[]{:S(2)}) %all-to-all-start) | async-done | bytes 2097184 | tf_op jit(solution)/shard_map/all_to_all | solution.py:57
  130.2 3.9 fusion.4
  134.1 107.7 %all-reduce.11.cloned.1.call-done = f32[128,1024]{0,1:T(8,128)} async-done(((f32[128,1024]{0,1:T(8,128)}), f32[128,1024]{0,1:T(8,128)}) %all-reduce.11.cloned.1.call-update) | async-done | bytes 524304 | tf_op jit(solution)/shard_map/psum | solution.py:65
  241.8 1.4 multiply_reduce_fusion.7
  243.2 105.8 %all-reduce.6 = (f32[]{:T(128)}, f32[]{:T(128)}) all-reduce(f32[]{:T(128)} %get-tuple-element.76, f32[]{:T(128)} %get-tuple-element.75), channel_id=1, replica_groups=mesh['blk'=32,'env'=16] {'blk','env'}, use_global_device_ids=true, to_apply=%region_8.9 | all-reduce | flops 2 | bytes 16 | tf_op jit(solution)/shard_map/psum | solution.py:69
  350.3 1.4 multiply_reduce_fusion.6
  351.7 99.5 %psum.87 = f32[]{:T(128)} all-reduce(f32[]{:T(128)} %get-tuple-element.113), channel_id=1, replica_groups=mesh['blk'=32,'env'=16] {'blk','env'}, use_global_device_ids=true, to_apply=%region_12.13 | all-reduce | flops 1 | bytes 8 | tf_op jit(solution)/shard_map/psum | solution.py:74
  451.9 29.6 %all_gather.10 = bf16[4096,64]{0,1:T(8,128)(2,1)S(1)} all-gather(bf16[128,64]{0,1:T(8,128)(2,1)S(1)} %multiply_convert_fusion.1), channel_id=1, replica_groups=mesh['blk'=32,'env'=16] {'blk'}, dimensions={0}, use_global_device_ids=true | all-gather | bytes 540672 | tf_op jit(solution)/shard_map/all_gather | solution.py:49
  481.6 1.6 broadcast.241.clone2.1
  483.2 37.2 %while.4 = (s32[]{:T(128)}, bf16[5120,64]{0,1:T(8,128)(2,1)S(1)}, s32[16,2]{0,1:T(2,128)S(1)}, bf16[16,1024,64]{1,2,0:T(8,128)(2,1)}, s32[]{:T(128)}) while((s32[]{:T(128)}, bf16[5120,64]{0,1:T(8,128)(2,1)S(1)}, s32[16,2]{0,1:T(2,128)S(1)}, bf16[16,1024,64]{1,2,0:T(8,128)(2,1)}, s32[]{:T(128)}) %tuple.79), condition=%wide.while_cond.1, body=%wide.while_body.1.sunk | while | flops 2 | bytes 1049181 | solution.py:54
  486.1 0.8 constant_dynamic-slice_fusion.15
  493.1 0.8 constant_dynamic-slice_fusion.15
  507.1 0.8 constant_dynamic-slice_fusion.15
  520.4 32.6 %all_to_all.45 = bf16[16,1,1024,64]{2,3,1,0:T(8,128)(2,1)} all-to-all(bf16[16,1,1024,64]{2,3,1,0:T(8,128)(2,1)} %bitcast.73), channel_id=1, replica_groups=mesh['blk'=32,'env'=16] {'env'}, dimensions={0} | all-to-all | bytes 4194304 | tf_op jit(solution)/shard_map/all_to_all | solution.py:57
  553.0 3.9 fusion.2
  557.0 108.5 %all-reduce.13.cloned.1.call-done = f32[128,1024]{0,1:T(8,128)} async-done(((f32[128,1024]{0,1:T(8,128)}), f32[128,1024]{0,1:T(8,128)}) %all-reduce.13.cloned.1.call-update) | async-done | bytes 524304 | tf_op jit(solution)/shard_map/psum | solution.py:65
  665.5 1.5 multiply_reduce_fusion.4
  666.9 105.8 %all-reduce.5 = (f32[]{:T(128)}, f32[]{:T(128)}) all-reduce(f32[]{:T(128)} %get-tuple-element.74, f32[]{:T(128)} %get-tuple-element.73), channel_id=1, replica_groups=mesh['blk'=32,'env'=16] {'blk','env'}, use_global_device_ids=true, to_apply=%region_15.16 | all-reduce | flops 2 | bytes 16 | tf_op jit(solution)/shard_map/psum | solution.py:69
  774.0 1.5 multiply_reduce_fusion.3
  775.4 99.5 %psum.91 = f32[]{:T(128)} all-reduce(f32[]{:T(128)} %get-tuple-element.111), channel_id=1, replica_groups=mesh['blk'=32,'env'=16] {'blk','env'}, use_global_device_ids=true, to_apply=%region_19.20 | all-reduce | flops 1 | bytes 8 | tf_op jit(solution)/shard_map/psum | solution.py:74
  875.7 29.6 %all_gather.11 = bf16[4096,64]{0,1:T(8,128)(2,1)S(1)} all-gather(bf16[128,64]{0,1:T(8,128)(2,1)S(1)} %multiply_convert_fusion), channel_id=1, replica_groups=mesh['blk'=32,'env'=16] {'blk'}, dimensions={0}, use_global_device_ids=true | all-gather | bytes 540672 | tf_op jit(solution)/shard_map/all_gather | solution.py:49
  905.4 1.6 broadcast.241.clone
  907.0 39.1 %while.5 = (s32[]{:T(128)}, bf16[5120,64]{0,1:T(8,128)(2,1)S(1)}, s32[16,2]{0,1:T(2,128)S(1)}, bf16[16,1024,64]{1,2,0:T(8,128)(2,1)}, s32[]{:T(128)}) while((s32[]{:T(128)}, bf16[5120,64]{0,1:T(8,128)(2,1)S(1)}, s32[16,2]{0,1:T(2,128)S(1)}, bf16[16,1024,64]{1,2,0:T(8,128)(2,1)}, s32[]{:T(128)}) %tuple.80), condition=%wide.while_cond.2, body=%wide.while_body.2.sunk | while | flops 2 | bytes 1049181 | solution.py:54
  907.6 0.8 constant_dynamic-slice_fusion.17
  910.1 0.8 constant_dynamic-slice_fusion.17
  912.5 0.8 constant_dynamic-slice_fusion.17
  915.0 0.8 constant_dynamic-slice_fusion.17
  917.4 0.8 constant_dynamic-slice_fusion.17
  919.9 0.8 constant_dynamic-slice_fusion.17
  922.3 0.8 constant_dynamic-slice_fusion.17
  924.8 0.8 constant_dynamic-slice_fusion.17
  927.2 0.8 constant_dynamic-slice_fusion.17
  929.7 0.8 constant_dynamic-slice_fusion.17
  932.1 0.8 constant_dynamic-slice_fusion.17
  934.6 0.8 constant_dynamic-slice_fusion.17
  937.0 0.8 constant_dynamic-slice_fusion.17
  939.4 0.8 constant_dynamic-slice_fusion.17
  941.9 0.8 constant_dynamic-slice_fusion.17
  944.3 0.8 constant_dynamic-slice_fusion.17
  946.1 32.6 %all_to_all.46 = bf16[16,1,1024,64]{2,3,1,0:T(8,128)(2,1)} all-to-all(bf16[16,1,1024,64]{2,3,1,0:T(8,128)(2,1)} %bitcast.71), channel_id=1, replica_groups=mesh['blk'=32,'env'=16] {'env'}, dimensions={0} | all-to-all | bytes 4194304 | tf_op jit(solution)/shard_map/all_to_all | solution.py:57
  978.7 3.9 fusion
  982.6 108.6 %all-reduce.15.cloned.1.call-done = f32[128,1024]{0,1:T(8,128)} async-done(((f32[128,1024]{0,1:T(8,128)}), f32[128,1024]{0,1:T(8,128)}) %all-reduce.15.cloned.1.call-update) | async-done | bytes 524304 | tf_op jit(solution)/shard_map/psum | solution.py:65
  1091.2 1.4 multiply_reduce_fusion.1
  1092.5 105.8 %all-reduce.4 = (f32[]{:T(128)}, f32[]{:T(128)}) all-reduce(f32[]{:T(128)} %get-tuple-element.72, f32[]{:T(128)} %get-tuple-element.71), channel_id=1, replica_groups=mesh['blk'=32,'env'=16] {'blk','env'}, use_global_device_ids=true, to_apply=%region_22.23 | all-reduce | flops 2 | bytes 16 | tf_op jit(solution)/shard_map/psum | solution.py:69
  1199.7 1.4 multiply_reduce_fusion
  1201.1 99.5 %psum.95 = f32[]{:T(128)} all-reduce(f32[]{:T(128)} %multiply_reduce_fusion), channel_id=1, replica_groups=mesh['blk'=32,'env'=16] {'blk','env'}, use_global_device_ids=true, to_apply=%region_26.27 | all-reduce | flops 1 | bytes 8 | tf_op jit(solution)/shard_map/psum | solution.py:74
  1301.9 1.4 broadcast_multiply_fusion
  (290 shorter events, 95.1 us)
Async XLA Ops:
  7.2 123.0 %copy-start = (bf16[1,1024,1024]{2,1,0:T(8,128)(2,1)S(1)}, bf16[1,1024,1024]{2,1,0:T(8,128)(2,1)}, u32[]{:S(2)}) copy-start(bf16[1,1024,1024]{2,1,0:T(8,128)(2,1)} %param.8) | copy-start | bytes 6291460
  90.3 39.8 %copy-start.1 = (bf16[128,1,1024]{2,0,1:T(8,128)(2,1)S(1)}, bf16[128,1,1024]{2,0,1:T(8,128)(2,1)}, u32[]{:S(2)}) copy-start(bf16[128,1,1024]{2,0,1:T(8,128)(2,1)} %param.7) | copy-start | bytes 786436
  90.3 39.8 %all-to-all-start = ((bf16[16,1,1024,64]{2,3,1,0:T(8,128)(2,1)}), bf16[16,1,1024,64]{2,3,1,0:T(8,128)(2,1)}, u32[]{:S(2)}, u32[]{:S(2)}) async-start(bf16[16,1,1024,64]{2,3,1,0:T(8,128)(2,1)} %bitcast.72), calls=%async_computation | async-start | bytes 4194304 | tf_op jit(solution)/shard_map/all_to_all | solution.py:57
  97.3 144.5 %all-reduce.11.cloned.1.call-start = ((), (), s32[]{:S(2)}) async-start(), calls=%async_computation.3 | async-start | bytes 1048576 | tf_op jit(solution)/shard_map/psum | solution.py:65
  130.2 111.6 %copy-start.2 = (f32[128,64]{0,1:T(8,128)S(1)}, f32[128,64]{0,1:T(8,128)}, u32[]{:S(2)}) copy-start(f32[128,64]{0,1:T(8,128)} %param.6) | copy-start | bytes 98308
  134.1 531.4 %all-reduce.13.cloned.1.call-start = ((), (), s32[]{:S(2)}) async-start(), calls=%async_computation.4 | async-start | bytes 1048576 | tf_op jit(solution)/shard_map/psum | solution.py:65
  556.9 534.2 %all-reduce.15.cloned.1.call-start = ((), (), s32[]{:S(2)}) async-start(), calls=%async_computation.5 | async-start | bytes 1048576 | tf_op jit(solution)/shard_map/psum | solution.py:65
Sparse Core Ops, SparseCore 0:
  134.2 107.5 all-reduce.10
  557.1 108.3 all-reduce.12
  982.7 108.4 all-reduce.14
where the time goes:
time: 1310 us
  blocking collectives  779 us (59%)
  waiting for transfers between devices  355 us (27%)
  local copies, waits for them, and re-layouts  119 us (9%)
  between operations  20.6 us (2%)
  other arithmetic  16.2 us (1%)
    psum x3, waiting for transfers between devices, per_device(): summed_all = lax.psum(partial_sum, 'env')  325 us
    psum x3, blocking collectives, per_device(): lax.psum((jnp.sum(vector * product), jnp.sum(vector * vector)), ('blk', '...  317 us
    psum x3, blocking collectives, per_device(): energy = lax.psum(jnp.sum(residual * residual), ('blk', 'env'))  299 us
    gather x288, local copies, waits for them, and re-layouts  112 us
    all_gather x3, blocking collectives, per_device(): every_row = lax.all_gather(rounded, 'blk', axis=0, tiled=True)  98.3 us
    all_to_all x2, blocking collectives, per_device(): lax.all_to_all(source_slabs, 'env', split_axis=0, concat_axis=3, tiled=True)  65.2 us
    all_to_all x1, waiting for transfers between devices, per_device(): lax.all_to_all(source_slabs, 'env', split_axis=0, concat_axis=3, tiled=True)  30.3 us
  transfers between devices with their start and end apart: 4, of which 4 were waited for; matrix products, arithmetic and copies ran while one was open for 0% of the time, Pallas kernels for 0%

commit v1 on v0

--- a/solution.py
+++ b/solution.py
@@ -62,7 +62,7 @@
         partial_sum = jnp.einsum(
             "trb,tbc->rc", channel_mix, env_right, preferred_element_type=jnp.float32
         )
-        summed_all = lax.psum(partial_sum, "env")
+        summed_all = jnp.sum(lax.all_gather(partial_sum, "env"), axis=0)
         product = lax.dynamic_slice_in_dim(
             summed_all, lax.axis_index("env") * col_width, col_width, 1
         )

time: 1310 us -> 1260 us (0.962)
  waiting for transfers between devices: 355 us -> 269 us
  local copies, waits for them, and re-layouts: 119 us -> 147 us
    psum x3 -> x0, waiting for transfers between devices: 325 us -> none  [per_device(): summed_all = lax.psum(partial_sum, 'env')]
    all_gather x0 -> x3, waiting for transfers between devices: none -> 239 us  [per_device(): summed_all = jnp.sum(lax.all_gather(partial_sum, 'env'), axis=0)]
    gather x288 -> x256, local copies, waits for them, and re-layouts: 112 us -> 136 us
    reduce_sum x0 -> x4, other arithmetic: none -> 13.4 us  [the longest x3 12.7 us: per_device(): summed_all = jnp.sum(lax.all_gather(partial_sum, 'env'), axis=0)]
where the time goes in v1:
time: 1260 us
  blocking collectives  780 us (62%)
  waiting for transfers between devices  269 us (21%)
  local copies, waits for them, and re-layouts  147 us (12%)
  other arithmetic  23.7 us (2%)
  between operations  20.7 us (2%)
    psum x3, blocking collectives, per_device(): lax.psum((jnp.sum(vector * product), jnp.sum(vector * vector)), ('blk', '...  313 us
    psum x3, blocking collectives, per_device(): energy = lax.psum(jnp.sum(residual * residual), ('blk', 'env'))  301 us
    all_gather x3, waiting for transfers between devices, per_device(): summed_all = jnp.sum(lax.all_gather(partial_sum, 'env'), axis=0)  239 us
    gather x256, local copies, waits for them, and re-layouts  136 us
    all_gather x3, blocking collectives, per_device(): every_row = lax.all_gather(rounded, 'blk', axis=0, tiled=True)  101 us
    all_to_all x2, blocking collectives, per_device(): lax.all_to_all(source_slabs, 'env', split_axis=0, concat_axis=3, tiled=True)  65.2 us
    all_to_all x1, waiting for transfers between devices, per_device(): lax.all_to_all(source_slabs, 'env', split_axis=0, concat_axis=3, tiled=True)  30.3 us
  transfers between devices with their start and end apart: 4, of which 4 were waited for; matrix products, arithmetic and copies ran while one was open for 0% of the time, Pallas kernels for 0%

profile of v1, /device:TPU:1, one launch (start us, length us, event | category | flops | bytes accessed | tf_op | source)
XLA Modules:
  0.0 1259.2 jit_solution(14174881208732632703)
XLA Ops:
  8.2 1.3 fusion.18
  11.8 1.4 multiply_reduce_fusion.8
  13.3 39.0 %all_gather.27 = bf16[4096,64]{0,1:T(8,128)(2,1)S(1)} all-gather(bf16[128,64]{0,1:T(8,128)(2,1)S(1)} %get-tuple-element.108), channel_id=1, replica_groups=mesh['blk'=32,'env'=16] {'blk'}, dimensions={0}, use_global_device_ids=true | all-gather | bytes 540672 | tf_op jit(solution)/shard_map/all_gather | solution.py:49
  52.3 1.6 broadcast.241.clone2
  53.9 39.1 %while.3 = (s32[]{:T(128)}, bf16[5120,64]{0,1:T(8,128)(2,1)S(1)}, s32[16,2]{0,1:T(2,128)S(1)}, bf16[16,1024,64]{1,2,0:T(8,128)(2,1)}, s32[]{:T(128)}) while((s32[]{:T(128)}, bf16[5120,64]{0,1:T(8,128)(2,1)S(1)}, s32[16,2]{0,1:T(2,128)S(1)}, bf16[16,1024,64]{1,2,0:T(8,128)(2,1)}, s32[]{:T(128)}) %tuple.62), condition=%wide.while_cond, body=%wide.while_body.sunk | while | flops 2 | bytes 1049181 | solution.py:54
  93.0 6.9 all-to-all-start
  102.5 30.3 %all-to-all-done = bf16[16,1,1024,64]{2,3,1,0:T(8,128)(2,1)} async-done(((bf16[16,1,1024,64]{2,3,1,0:T(8,128)(2,1)}), bf16[16,1,1024,64]{2,3,1,0:T(8,128)(2,1)}, u32[]{:S(2)}, u32[]{:S(2)}) %all-to-all-start) | async-done | bytes 2097184 | tf_op jit(solution)/shard_map/all_to_all | solution.py:57
  132.8 3.6 fusion.4
  136.6 79.2 %all-gather.7.cloned.1.call-done = f32[2048,1024]{1,0:T(8,128)} async-done(((f32[128,1024]{1,0:T(8,128)}), f32[2048,1024]{1,0:T(8,128)}) %all-gather.7.cloned.1.call-update) | async-done | bytes 8388624 | tf_op jit(solution)/shard_map/all_gather | solution.py:65
  215.7 4.2 reduce_sum.158
  220.7 104.2 %all-reduce.6 = (f32[]{:T(128)}, f32[]{:T(128)}) all-reduce(f32[]{:T(128)} %get-tuple-element.103, f32[]{:T(128)} %get-tuple-element.107), channel_id=1, replica_groups=mesh['blk'=32,'env'=16] {'blk','env'}, use_global_device_ids=true, to_apply=%region_8.9 | all-reduce | flops 2 | bytes 16 | tf_op jit(solution)/shard_map/psum | solution.py:69
  326.8 100.3 %psum.65 = f32[]{:T(128)} all-reduce(f32[]{:T(128)} %get-tuple-element.101), channel_id=1, replica_groups=mesh['blk'=32,'env'=16] {'blk','env'}, use_global_device_ids=true, to_apply=%region_12.13 | all-reduce | flops 1 | bytes 8 | tf_op jit(solution)/shard_map/psum | solution.py:74
  427.8 31.2 %all_gather.30 = bf16[4096,64]{1,0:T(8,128)(2,1)S(1)} all-gather(bf16[128,64]{1,0:T(8,128)(2,1)S(1)} %multiply_convert_fusion.1), channel_id=1, replica_groups=mesh['blk'=32,'env'=16] {'blk'}, dimensions={0}, use_global_device_ids=true | all-gather | bytes 540672 | tf_op jit(solution)/shard_map/all_gather | solution.py:49
  459.1 1.3 concatenate.16
  460.3 1.6 broadcast.241.clone2.1
  462.0 49.0 %while.4 = (s32[]{:T(128)}, bf16[5120,64]{1,0:T(8,128)(2,1)}, s32[16,2]{0,1:T(2,128)S(1)}, bf16[16,1024,64]{1,2,0:T(8,128)(2,1)}, s32[]{:T(128)}) while((s32[]{:T(128)}, bf16[5120,64]{1,0:T(8,128)(2,1)}, s32[16,2]{0,1:T(2,128)S(1)}, bf16[16,1024,64]{1,2,0:T(8,128)(2,1)}, s32[]{:T(128)}) %tuple.77), condition=%wide.while_cond.1, body=%wide.while_body.1.sunk | while | flops 2 | bytes 787037 | solution.py:54
  462.6 1.7 dynamic-slice_bitcast_fusion.4
  465.6 1.7 dynamic-slice_bitcast_fusion.4
  468.7 1.7 dynamic-slice_bitcast_fusion.4
  471.7 1.7 dynamic-slice_bitcast_fusion.4
  474.8 1.7 dynamic-slice_bitcast_fusion.4
  477.9 1.7 dynamic-slice_bitcast_fusion.4
  480.9 1.7 dynamic-slice_bitcast_fusion.4
  484.0 1.7 dynamic-slice_bitcast_fusion.4
  487.0 1.7 dynamic-slice_bitcast_fusion.4
  490.1 1.7 dynamic-slice_bitcast_fusion.4
  493.2 1.7 dynamic-slice_bitcast_fusion.4
  496.2 1.7 dynamic-slice_bitcast_fusion.4
  499.3 1.7 dynamic-slice_bitcast_fusion.4
  502.3 1.7 dynamic-slice_bitcast_fusion.4
  505.4 1.7 dynamic-slice_bitcast_fusion.4
  508.5 1.7 dynamic-slice_bitcast_fusion.4
  510.9 32.6 %all_to_all.45 = bf16[16,1,1024,64]{2,3,1,0:T(8,128)(2,1)} all-to-all(bf16[16,1,1024,64]{2,3,1,0:T(8,128)(2,1)} %bitcast.76), channel_id=1, replica_groups=mesh['blk'=32,'env'=16] {'env'}, dimensions={0} | all-to-all | bytes 4194304 | tf_op jit(solution)/shard_map/all_to_all | solution.py:57
  543.5 3.6 fusion.2
  547.2 80.0 %all-gather.9.cloned.1.call-done = f32[2048,1024]{1,0:T(8,128)} async-done(((f32[128,1024]{1,0:T(8,128)}), f32[2048,1024]{1,0:T(8,128)}) %all-gather.9.cloned.1.call-update) | async-done | bytes 8388624 | tf_op jit(solution)/shard_map/all_gather | solution.py:65
  627.2 4.2 reduce_sum.162
  632.1 104.2 %all-reduce.5 = (f32[]{:T(128)}, f32[]{:T(128)}) all-reduce(f32[]{:T(128)} %get-tuple-element.62, f32[]{:T(128)} %get-tuple-element.61), channel_id=1, replica_groups=mesh['blk'=32,'env'=16] {'blk','env'}, use_global_device_ids=true, to_apply=%region_15.16 | all-reduce | flops 2 | bytes 16 | tf_op jit(solution)/shard_map/psum | solution.py:69
  738.3 100.3 %psum.68 = f32[]{:T(128)} all-reduce(f32[]{:T(128)} %get-tuple-element.98), channel_id=1, replica_groups=mesh['blk'=32,'env'=16] {'blk','env'}, use_global_device_ids=true, to_apply=%region_19.20 | all-reduce | flops 1 | bytes 8 | tf_op jit(solution)/shard_map/psum | solution.py:74
  839.3 31.2 %all_gather.33 = bf16[4096,64]{1,0:T(8,128)(2,1)S(1)} all-gather(bf16[128,64]{1,0:T(8,128)(2,1)S(1)} %multiply_convert_fusion), channel_id=1, replica_groups=mesh['blk'=32,'env'=16] {'blk'}, dimensions={0}, use_global_device_ids=true | all-gather | bytes 540672 | tf_op jit(solution)/shard_map/all_gather | solution.py:49
  870.5 1.3 concatenate.17
  871.8 1.6 broadcast.241.clone
  873.4 48.9 %while.5 = (s32[]{:T(128)}, bf16[5120,64]{1,0:T(8,128)(2,1)}, s32[16,2]{0,1:T(2,128)S(1)}, bf16[16,1024,64]{1,2,0:T(8,128)(2,1)}, s32[]{:T(128)}) while((s32[]{:T(128)}, bf16[5120,64]{1,0:T(8,128)(2,1)}, s32[16,2]{0,1:T(2,128)S(1)}, bf16[16,1024,64]{1,2,0:T(8,128)(2,1)}, s32[]{:T(128)}) %tuple.78), condition=%wide.while_cond.2, body=%wide.while_body.2.sunk | while | flops 2 | bytes 787037 | solution.py:54
  874.0 1.7 dynamic-slice_bitcast_fusion.5
  877.1 1.7 dynamic-slice_bitcast_fusion.5
  880.1 1.7 dynamic-slice_bitcast_fusion.5
  883.2 1.7 dynamic-slice_bitcast_fusion.5
  886.2 1.7 dynamic-slice_bitcast_fusion.5
  889.3 1.7 dynamic-slice_bitcast_fusion.5
  892.3 1.7 dynamic-slice_bitcast_fusion.5
  895.4 1.7 dynamic-slice_bitcast_fusion.5
  898.5 1.7 dynamic-slice_bitcast_fusion.5
  901.5 1.7 dynamic-slice_bitcast_fusion.5
  904.6 1.7 dynamic-slice_bitcast_fusion.5
  907.7 1.7 dynamic-slice_bitcast_fusion.5
  910.7 1.7 dynamic-slice_bitcast_fusion.5
  913.8 1.7 dynamic-slice_bitcast_fusion.5
  916.8 1.7 dynamic-slice_bitcast_fusion.5
  919.9 1.7 dynamic-slice_bitcast_fusion.5
  922.3 32.6 %all_to_all.46 = bf16[16,1,1024,64]{2,3,1,0:T(8,128)(2,1)} all-to-all(bf16[16,1,1024,64]{2,3,1,0:T(8,128)(2,1)} %bitcast.74), channel_id=1, replica_groups=mesh['blk'=32,'env'=16] {'env'}, dimensions={0} | all-to-all | bytes 4194304 | tf_op jit(solution)/shard_map/all_to_all | solution.py:57
  954.9 3.5 fusion
  958.6 79.9 %all-gather.11.cloned.1.call-done = f32[2048,1024]{1,0:T(8,128)} async-done(((f32[128,1024]{1,0:T(8,128)}), f32[2048,1024]{1,0:T(8,128)}) %all-gather.11.cloned.1.call-update) | async-done | bytes 8388624 | tf_op jit(solution)/shard_map/all_gather | solution.py:65
  1038.6 4.2 reduce_sum.166
  1043.5 104.2 %all-reduce.4 = (f32[]{:T(128)}, f32[]{:T(128)}) all-reduce(f32[]{:T(128)} %get-tuple-element.60, f32[]{:T(128)} %get-tuple-element.59), channel_id=1, replica_groups=mesh['blk'=32,'env'=16] {'blk','env'}, use_global_device_ids=true, to_apply=%region_22.23 | all-reduce | flops 2 | bytes 16 | tf_op jit(solution)/shard_map/psum | solution.py:69
  1149.7 100.3 %psum.71 = f32[]{:T(128)} all-reduce(f32[]{:T(128)} %multiply_reduce_fusion), channel_id=1, replica_groups=mesh['blk'=32,'env'=16] {'blk','env'}, use_global_device_ids=true, to_apply=%region_26.27 | all-reduce | flops 1 | bytes 8 | tf_op jit(solution)/shard_map/psum | solution.py:74
  (266 shorter events, 94.4 us)
Async XLA Ops:
  7.2 125.7 %copy-start = (bf16[1,1024,1024]{2,1,0:T(8,128)(2,1)S(1)}, bf16[1,1024,1024]{2,1,0:T(8,128)(2,1)}, u32[]{:S(2)}) copy-start(bf16[1,1024,1024]{2,1,0:T(8,128)(2,1)} %param.8) | copy-start | bytes 6291460
  93.0 39.8 %copy-start.1 = (bf16[128,1,1024]{2,0,1:T(8,128)(2,1)S(1)}, bf16[128,1,1024]{2,0,1:T(8,128)(2,1)}, u32[]{:S(2)}) copy-start(bf16[128,1,1024]{2,0,1:T(8,128)(2,1)} %param.7) | copy-start | bytes 786436
  93.0 39.8 %all-to-all-start = ((bf16[16,1,1024,64]{2,3,1,0:T(8,128)(2,1)}), bf16[16,1,1024,64]{2,3,1,0:T(8,128)(2,1)}, u32[]{:S(2)}, u32[]{:S(2)}) async-start(bf16[16,1,1024,64]{2,3,1,0:T(8,128)(2,1)} %bitcast.75), calls=%async_computation | async-start | bytes 4194304 | tf_op jit(solution)/shard_map/all_to_all | solution.py:57
  99.9 115.8 %all-gather.7.cloned.1.call-start = ((), (), s32[]{:S(2)}) async-start(), calls=%async_computation.3 | async-start | bytes 8912896 | tf_op jit(solution)/shard_map/all_gather | solution.py:65
  132.8 3.6 copy-start.2
  136.4 490.8 %all-gather.9.cloned.1.call-start = ((), (), s32[]{:S(2)}) async-start(), calls=%async_computation.4 | async-start | bytes 8912896 | tf_op jit(solution)/shard_map/all_gather | solution.py:65
  547.1 491.4 %all-gather.11.cloned.1.call-start = ((), (), s32[]{:S(2)}) async-start(), calls=%async_computation.5 | async-start | bytes 8912896 | tf_op jit(solution)/shard_map/all_gather | solution.py:65
Sparse Core Ops, SparseCore 0:
  136.5 79.1 all-gather.6
  547.2 79.8 all-gather.8
  958.6 79.8 all-gather.10
